TPU v7x, 256 devices: a whole 4x4x8 slice. The times are simulated.
256 devices in a mesh: trow: 16 (over x, y), tcol: 8 (over z), rep: 2 (over core).
Axes of the slice: x: 4, y: 4, z: 8, core: 2. Of those that a mesh axis runs over, the one named last changes fastest.
Arguments:
- users: float32 [131072, 128], P(('trow', 'tcol'))
- items: float32 [65536, 128], P(('tcol', 'trow'))
- ratings: bfloat16 [16, 8, 2, 64, 128, 128], P('trow', 'tcol', 'rep'), may hold values from -6 to 6
- row_mask: int32 [16, 8, 2, 64, 128], P('trow', 'tcol', 'rep'), may hold values 0 or 1
- col_mask: int32 [16, 8, 2, 64, 128], P('trow', 'tcol', 'rep'), may hold values 0 or 1
- row_slots: int32 [16, 8, 2, 64], P('trow', 'tcol', 'rep'), may hold values from 0 to 31, as said below
- col_slots: int32 [16, 8, 2, 64], P('trow', 'tcol', 'rep'), may hold values from 0 to 31, as said below
- send_users: int32 [16, 8, 2, 8, 4], P('trow', 'tcol', 'rep'), may hold values from 0 to 7, as said below
- send_items: int32 [16, 8, 2, 16, 2], P('trow', 'tcol', 'rep'), may hold values from 0 to 3, as said below
Outputs:
- users_out: float32 [131072, 128], P(('trow', 'tcol'))
- items_out: float32 [65536, 128], P(('tcol', 'trow'))
Inputs may be any that keep to these rules, and one draw needn't show every extreme that they name: `send_users`: distinct within each row of the last dimension. `send_items`: distinct within each row of the last dimension. `row_slots`: every slot is named by some tile of each device. `col_slots`: every slot is named by some tile of each device.
All inputs are finite; a program needn't handle non-finite values. No bound on the sum of `row_mask` or of `col_mask` on one device may be relied on, other than what follows from the above.
Results may differ from a plain program's by a relative error of at most 0.02.
Values may be sent and summed in bfloat16 or wider, within the bound.
A program may use at most 64 MiB of HBM per device.

v0:
```python
import jax
import jax.numpy as jnp
from jax import lax
from jax.sharding import PartitionSpec as P

ITERS = 2


def precondition(gradient, gramian):
    factor = jnp.linalg.cholesky(gramian)
    return jax.scipy.linalg.cho_solve((factor, True), gradient.T).T


def pool_sum(index_list, terms, pool_count):
    onehot = (
        lax.broadcasted_iota(jnp.int32, (pool_count, index_list.shape[0]), 0) == index_list[None, :]
    ).astype(jnp.bfloat16)
    flat = terms.reshape(terms.shape[0], -1)
    upper = flat.astype(jnp.bfloat16)
    lower = (flat - upper.astype(jnp.float32)).astype(jnp.bfloat16)
    return jnp.dot(onehot, upper, preferred_element_type=jnp.float32) + jnp.dot(
        onehot, lower, preferred_element_type=jnp.float32
    )


def on_device(
    users, items, ratings, row_mask, col_mask, row_slots, col_slots, send_users, send_items
):
    n_trow = lax.axis_size("trow")
    n_tcol = lax.axis_size("tcol")
    n_rep = lax.axis_size("rep")
    tile_size = ratings.shape[-1]
    rank_width = users.shape[1]
    tile_count = ratings.shape[3]
    own_users = users.shape[0] // tile_size
    own_items = items.shape[0] // tile_size
    user_cap = send_users.shape[-1]
    item_cap = send_items.shape[-1]
    ratings_local = ratings.reshape(tile_count, tile_size, tile_size)
    weights = (
        row_mask.reshape(tile_count, tile_size)[:, :, None]
        * col_mask.reshape(tile_count, tile_size)[:, None, :]
    ).astype(jnp.float32)
    row_slot_list = row_slots.reshape(-1)
    col_slot_list = col_slots.reshape(-1)
    user_sends = send_users.reshape(n_tcol, -1)
    item_sends = send_items.reshape(n_trow, -1)
    user_received = lax.all_to_all(
        user_sends, "tcol", split_axis=0, concat_axis=0, tiled=True
    ).reshape(-1)
    item_received = lax.all_to_all(
        item_sends, "trow", split_axis=0, concat_axis=0, tiled=True
    ).reshape(-1)
    row_list = row_slot_list // user_cap * own_users + user_received[row_slot_list]
    col_list = col_slot_list // item_cap * own_items + item_received[col_slot_list]
    all_users = own_users * tile_size * n_trow * n_tcol
    all_items = own_items * tile_size * n_trow * n_tcol
    user_coef = 2.0 * all_items * own_users / (tile_size * tile_count * n_rep)
    item_coef = 2.0 * all_users * own_items / (tile_size * tile_count * n_rep)
    for iteration in range(ITERS):
        gram_users, gram_items = lax.psum(
            (
                jnp.dot(
                    users.T,
                    users,
                    precision=lax.Precision.HIGHEST,
                    preferred_element_type=jnp.float32,
                ),
                jnp.dot(
                    items.T,
                    items,
                    precision=lax.Precision.HIGHEST,
                    preferred_element_type=jnp.float32,
                ),
            ),
            ("trow", "tcol"),
        )
        user_half = users.astype(jnp.bfloat16).reshape(own_users, tile_size, rank_width)
        item_half = items.astype(jnp.bfloat16).reshape(own_items, tile_size, rank_width)
        user_pool = lax.all_gather(user_half, "tcol", axis=0, tiled=True)
        item_pool = lax.all_gather(item_half, "trow", axis=0, tiled=True)
        x_tiles = user_pool[row_list]
        y_tiles = item_pool[col_list]
        predicted = jnp.einsum("tar,tbr->tab", x_tiles, y_tiles, preferred_element_type=jnp.float32)
        errors = (weights * (predicted - ratings_local.astype(jnp.float32))).astype(jnp.bfloat16)
        user_terms = jnp.einsum("tab,tbr->tar", errors, y_tiles, preferred_element_type=jnp.float32)
        item_terms = jnp.einsum("tab,tar->tbr", errors, x_tiles, preferred_element_type=jnp.float32)
        user_pooled = pool_sum(row_list, user_terms, user_pool.shape[0])
        item_pooled = pool_sum(col_list, item_terms, item_pool.shape[0])
        user_grad = lax.psum_scatter(user_pooled, "tcol", scatter_dimension=0, tiled=True)
        item_grad = lax.psum_scatter(item_pooled, "trow", scatter_dimension=0, tiled=True)
        user_grad, item_grad = lax.psum((user_grad, item_grad), "rep")
        new_users = users - user_coef * precondition(user_grad.reshape(-1, rank_width), gram_items)
        new_items = items - item_coef * precondition(item_grad.reshape(-1, rank_width), gram_users)
        users, items = (new_users, new_items)
    return (users, items)


def solution(mesh):
    return jax.shard_map(
        on_device,
        mesh=mesh,
        in_specs=(
            P(("trow", "tcol"), None),
            P(("tcol", "trow"), None),
            P("trow", "tcol", "rep", None, None, None),
            P("trow", "tcol", "rep", None, None),
            P("trow", "tcol", "rep", None, None),
            P("trow", "tcol", "rep", None),
            P("trow", "tcol", "rep", None),
            P("trow", "tcol", "rep", None, None),
            P("trow", "tcol", "rep", None, None),
        ),
        out_specs=(P(("trow", "tcol"), None), P(("tcol", "trow"), None)),
        check_vma=False,
    )
```

profile of v0, /device:TPU:1, one launch (start us, length us, event | category | flops | bytes accessed | tf_op | source)
XLA Modules:
  0.0 1075.5 jit_solution(2654260133140196737)
XLA Ops:
  7.2 1.8 convert_element_type.69
  9.1 1.6 convert_element_type.70
  10.7 1.3 copy.48
  12.1 7.6 all-to-all-start.1
  21.0 1.3 copy.47
  22.3 3.7 all-to-all-done.1
  26.1 8.2 all-to-all-start
  36.4 4.4 all-to-all-done
  42.3 9.4 all-gather.5.cloned.1.call-done
  51.7 3.7 gather_fusion.1
  55.4 50.8 %all-gather.7.cloned.1.call-done = bf16[64,128,128]{2,1,0:T(8,128)(2,1)} async-done(((bf16[4,128,128]{2,1,0:T(8,128)(2,1)}), bf16[64,128,128]{2,1,0:T(8,128)(2,1)}) %all-gather.7.cloned.1.call-update) | async-done | bytes 2097168 | tf_op jit(solution)/shard_map/all_gather | solution.py:81
  106.3 2.5 gather_fusion.3
  108.9 4.1 fusion.1
  114.4 2.8 fusion.9
  117.2 4.9 convolution_add_fusion.2
  122.3 2.3 fusion.59
  124.6 2.8 fusion.8
  127.4 4.9 convolution_add_fusion.3
  134.5 1.6 fusion.60
  137.4 98.5 %all-reduce.13.cloned.1.call-done = f32[64,16384]{1,0:T(8,128)} async-done(((f32[64,16384]{1,0:T(8,128)}), f32[64,16384]{1,0:T(8,128)}) %all-reduce.13.cloned.1.call-update) | async-done | bytes 4194320
  237.9 55.8 %reduce-scatter.3.cloned.1.call-done = f32[8,16384]{1,0:T(8,128)} async-done(((f32[64,16384]{1,0:T(8,128)}), f32[8,16384]{1,0:T(8,128)}) %reduce-scatter.3.cloned.1.call-update) | async-done | bytes 524304 | tf_op jit(solution)/shard_map/reduce_scatter | solution.py:90
  293.7 1.9 reshape.380
  296.1 209.1 %all-reduce.19.cloned.1.call-done = (f32[128,128]{0,1:T(8,128)}, f32[128,128]{0,1:T(8,128)}) async-done(((f32[128,128]{0,1:T(8,128)}, f32[128,128]{0,1:T(8,128)}), (f32[128,128]{0,1:T(8,128)}, f32[128,128]{0,1:T(8,128)})) %all-reduce.19.cloned.1.call-update) | async-done | bytes 131088 | tf_op jit(solution)/shard_map/psum | solution.py:61
  508.0 11.7 %cholesky.74 = f32[128,128]{1,0:T(8,128)S(1)} custom-call(f32[128,128]{1,0:T(8,128)S(1)} %get-tuple-element.24), custom_call_target="Cholesky" | custom-call | tf_op jit(solution)/shard_map/jit(cholesky)/cholesky | solution.py:10
  521.1 9.8 custom-call.14
  530.9 10.3 all-reduce.23.cloned.1.call-done
  541.2 1.7 fusion.41
  545.1 11.7 %cholesky.85 = f32[128,128]{1,0:T(8,128)S(1)} custom-call(f32[128,128]{1,0:T(8,128)S(1)} %get-tuple-element.23), custom_call_target="Cholesky" | custom-call | tf_op jit(solution)/shard_map/jit(cholesky)/cholesky | solution.py:10
  558.1 9.8 custom-call.15
  572.0 10.9 %all-gather.9.cloned.1.call-done = bf16[64,128,128]{2,1,0:T(8,128)(2,1)} async-done(((bf16[8,128,128]{2,1,0:T(8,128)(2,1)}), bf16[64,128,128]{2,1,0:T(8,128)(2,1)}) %all-gather.9.cloned.1.call-update) | async-done | bytes 2097168 | tf_op jit(solution)/shard_map/all_gather | solution.py:80
  582.9 3.7 gather_fusion.4
  586.7 50.5 %all-gather.11.cloned.1.call-done = bf16[64,128,128]{2,1,0:T(8,128)(2,1)} async-done(((bf16[4,128,128]{2,1,0:T(8,128)(2,1)}), bf16[64,128,128]{2,1,0:T(8,128)(2,1)}) %all-gather.11.cloned.1.call-update) | async-done | bytes 2097168 | tf_op jit(solution)/shard_map/all_gather | solution.py:81
  637.2 2.5 gather_fusion.5
  639.7 4.1 fusion.3
  645.2 2.8 fusion.11
  648.0 4.9 convolution_add_fusion
  653.0 2.3 fusion.63
  655.3 2.8 fusion.10
  658.1 4.9 convolution_add_fusion.1
  663.2 187.3 %all-reduce.17.cloned.1.call-done = (f32[128,128]{0,1:T(8,128)}, f32[128,128]{0,1:T(8,128)}) async-done(((f32[128,128]{0,1:T(8,128)}, f32[128,128]{0,1:T(8,128)}), (f32[128,128]{0,1:T(8,128)}, f32[128,128]{0,1:T(8,128)})) %all-reduce.17.cloned.1.call-update) | async-done | bytes 131088 | tf_op jit(solution)/shard_map/psum | solution.py:61
  852.4 11.7 %cholesky.96 = f32[128,128]{1,0:T(8,128)S(1)} custom-call(f32[128,128]{1,0:T(8,128)S(1)} %fusion.35), custom_call_target="Cholesky" | custom-call | tf_op jit(solution)/shard_map/jit(cholesky)/cholesky | solution.py:10
  864.8 104.5 %all-reduce.15.cloned.1.call-done = f32[64,16384]{1,0:T(8,128)} async-done(((f32[64,16384]{1,0:T(8,128)}), f32[64,16384]{1,0:T(8,128)}) %all-reduce.15.cloned.1.call-update) | async-done | bytes 4194320
  971.4 56.1 %reduce-scatter.5.cloned.1.call-done = f32[8,16384]{1,0:T(8,128)} async-done(((f32[64,16384]{1,0:T(8,128)}), f32[8,16384]{1,0:T(8,128)}) %reduce-scatter.5.cloned.1.call-update) | async-done | bytes 524304 | tf_op jit(solution)/shard_map/reduce_scatter | solution.py:90
  1027.5 1.9 reshape.387
  1030.1 9.8 custom-call.16
  1040.0 11.7 %cholesky.107 = f32[128,128]{1,0:T(8,128)S(1)} custom-call(f32[128,128]{1,0:T(8,128)S(1)} %fusion.31), custom_call_target="Cholesky" | custom-call | tf_op jit(solution)/shard_map/jit(cholesky)/cholesky | solution.py:10
  1053.2 10.0 custom-call.17
  1063.3 1.7 fusion.33
  (111 shorter events, 35.1 us)
Async XLA Ops:
  7.2 35.1 %copy-start.12 = (s32[1,1,1,64]{3,2,1,0:T(1,128)S(1)}, s32[1,1,1,64]{3,2,1,0:T(1,128)}, u32[]{:S(2)}) copy-start(s32[1,1,1,64]{3,2,1,0:T(1,128)} %param.19) | copy-start | bytes 772
  7.2 29.1 %copy-start.11 = (s32[1,1,1,64]{3,2,1,0:T(1,128)S(1)}, s32[1,1,1,64]{3,2,1,0:T(1,128)}, u32[]{:S(2)}) copy-start(s32[1,1,1,64]{3,2,1,0:T(1,128)} %param.20) | copy-start | bytes 772
  7.2 44.5 %all-gather.5.cloned.1.call-start = ((), (), s32[]{:S(2)}) async-start(), calls=%async_computation.4 | async-start | bytes 2359296 | tf_op jit(solution)/shard_map/all_gather | solution.py:80
  9.0 97.3 %all-gather.7.cloned.1.call-start = ((), (), s32[]{:S(2)}) async-start(), calls=%async_computation.5 | async-start | bytes 2228224 | tf_op jit(solution)/shard_map/all_gather | solution.py:81
  12.1 14.0 %all-to-all-start.1 = ((s32[16,1,2]{2,1,0:T(1,128)}), s32[16,1,2]{2,1,0:T(1,128)S(1)}, u32[]{:S(2)}, u32[]{:S(2)}) async-start(s32[16,1,2]{2,1,0:T(1,128)} %copy.48), calls=%async_computation.1 | async-start | bytes 16384 | tf_op jit(solution)/shard_map/all_to_all | solution.py:51
  26.1 14.7 %all-to-all-start = ((s32[8,1,4]{2,1,0:T(1,128)}), s32[8,1,4]{2,1,0:T(1,128)S(1)}, u32[]{:S(2)}, u32[]{:S(2)}) async-start(s32[8,1,4]{2,1,0:T(1,128)} %copy.47), calls=%async_computation | async-start | bytes 8192 | tf_op jit(solution)/shard_map/all_to_all | solution.py:48
  34.3 201.6 %all-reduce.13.cloned.1.call-start = ((), (), s32[]{:S(2)}) async-start(), calls=%async_computation.10 | async-start | bytes 8388608
  55.4 53.4 %copy-start.9 = (s32[1,1,1,64,128]{4,3,2,1,0:T(8,128)S(1)}, s32[1,1,1,64,128]{4,3,2,1,0:T(8,128)}, u32[]{:S(2)}) copy-start(s32[1,1,1,64,128]{4,3,2,1,0:T(8,128)} %param.18) | copy-start | bytes 98308
  55.4 53.4 %copy-start.10 = (s32[1,1,1,64,128]{4,3,2,1,0:T(8,128)S(1)}, s32[1,1,1,64,128]{4,3,2,1,0:T(8,128)}, u32[]{:S(2)}) copy-start(s32[1,1,1,64,128]{4,3,2,1,0:T(8,128)} %param.17) | copy-start | bytes 98308
  108.9 4.1 copy-start.1
  113.0 1.4 copy-start.2
  122.1 171.6 %reduce-scatter.3.cloned.1.call-start = ((), (), s32[]{:S(2)}) async-start(), calls=%async_computation.6 | async-start | bytes 4718592 | tf_op jit(solution)/shard_map/reduce_scatter | solution.py:90
  132.3 1.0 copy-start.5
  132.3 2.2 copy-start.4
  132.3 3.9 copy-start.13
  132.3 372.9 %all-reduce.19.cloned.1.call-start = ((), (), s32[]{:S(2)}) async-start(), calls=%async_computation.13 | async-start | bytes 262144 | tf_op jit(solution)/shard_map/psum | solution.py:61
  136.1 405.1 %all-reduce.23.cloned.1.call-start = ((), (), s32[]{:S(2)}) async-start(), calls=%async_computation.15 | async-start | bytes 1572864 | tf_op jit(solution)/shard_map/psum | solution.py:92
  295.6 287.3 %all-gather.9.cloned.1.call-start = ((), (), s32[]{:S(2)}) async-start(), calls=%async_computation.7 | async-start | bytes 2359296 | tf_op jit(solution)/shard_map/all_gather | solution.py:80
  541.2 26.7 %copy-start.7 = (f32[128,512]{0,1:T(8,128)S(1)}, f32[128,512]{0,1:T(8,128)}, u32[]{:S(2)}) copy-start(f32[128,512]{0,1:T(8,128)} %get-tuple-element.18) | copy-start | bytes 786436
  544.4 92.8 %all-gather.11.cloned.1.call-start = ((), (), s32[]{:S(2)}) async-start(), calls=%async_computation.8 | async-start | bytes 2228224 | tf_op jit(solution)/shard_map/all_gather | solution.py:81
  569.5 281.0 %all-reduce.17.cloned.1.call-start = ((), (), s32[]{:S(2)}) async-start(), calls=%async_computation.12 | async-start | bytes 262144 | tf_op jit(solution)/shard_map/psum | solution.py:61
  571.8 397.6 %all-reduce.15.cloned.1.call-start = ((), (), s32[]{:S(2)}) async-start(), calls=%async_computation.11 | async-start | bytes 8388608
  639.7 4.1 copy-start
  643.9 1.4 copy-start.3
  652.9 374.5 %reduce-scatter.5.cloned.1.call-start = ((), (), s32[]{:S(2)}) async-start(), calls=%async_computation.9 | async-start | bytes 4718592 | tf_op jit(solution)/shard_map/reduce_scatter | solution.py:90
  663.0 400.3 %all-reduce.21.cloned.1.call-start = ((), (), s32[]{:S(2)}) async-start(), calls=%async_computation.14 | async-start | bytes 1572864 | tf_op jit(solution)/shard_map/psum | solution.py:92
  850.6 189.4 %copy-start.6 = (f32[128,128]{0,1:T(8,128)S(1)}, f32[128,128]{0,1:T(8,128)}, u32[]{:S(2)}) copy-start(f32[128,128]{0,1:T(8,128)} %get-tuple-element.12) | copy-start | bytes 196612
  1063.2 3.3 copy-start.8
Sparse Core Ops, SparseCore 0:
  10.4 41.2 all-gather.4
  54.7 51.5 all-gather.6
  122.2 113.6 all-reduce.12
  238.3 55.3 reduce-scatter.2
  299.1 206.1 all-reduce.18
  508.5 32.6 all-reduce.22
  544.5 38.3 all-gather.8
  585.9 51.1 all-gather.10
  642.7 207.7 all-reduce.16
  854.1 115.2 all-reduce.14
  972.1 55.3 reduce-scatter.4
  1030.7 29.7 all-reduce.20
where the time goes:
time: 1080 us
  waiting for transfers between devices  852 us (79%)
  other arithmetic  99.6 us (9%)
  matrix products  56.4 us (5%)
  local copies, waits for them, and re-layouts  34.4 us (3%)
  starting transfers between devices  17.6 us (2%)
  between operations  15.7 us (1%)
    psum x2, waiting for transfers between devices, on_device(): lax.psum((jnp.dot(users.T, users, precision=lax.Precision.HIGHEST, prefer...  396 us
    unnamed x14, waiting for transfers between devices  203 us
    reduce_scatter x2, waiting for transfers between devices, on_device(): lax.psum_scatter(user_pooled, 'tcol', scatter_dimension=0, tiled=True)  112 us
    all_gather x2, waiting for transfers between devices, on_device(): item_pool = lax.all_gather(item_half, 'trow', axis=0, tiled=True)  101 us
    another operation x12, other arithmetic, precondition(): factor = jnp.linalg.cholesky(gramian)  49.7 us
    another operation x8, other arithmetic, precondition(): return jax.scipy.linalg.cho_solve((factor, True), gradient.T).T  42.1 us
  transfers between devices with their start and end apart: 14, of which 13 were waited for; matrix products, arithmetic and copies ran while one was open for 15% of the time, Pallas kernels for 0%

commit v1 on v0

--- a/solution.py
+++ b/solution.py
@@ -78,7 +78,9 @@
         user_half = users.astype(jnp.bfloat16).reshape(own_users, tile_size, rank_width)
         item_half = items.astype(jnp.bfloat16).reshape(own_items, tile_size, rank_width)
         user_pool = lax.all_gather(user_half, "tcol", axis=0, tiled=True)
-        item_pool = lax.all_gather(item_half, "trow", axis=0, tiled=True)
+        item_pool = jnp.concatenate(
+            lax.all_to_all(jnp.stack([item_half] * lax.axis_size("trow")), "trow", 0, 0), axis=0
+        )
         x_tiles = user_pool[row_list]
         y_tiles = item_pool[col_list]
         predicted = jnp.einsum("tar,tbr->tab", x_tiles, y_tiles, preferred_element_type=jnp.float32)

time: 1080 us -> 1000 us (0.926)
  waiting for transfers between devices: 852 us -> 754 us
    all_gather x2 -> x0, waiting for transfers between devices: 101 us -> none  [on_device(): item_pool = lax.all_gather(item_half, 'trow', axis=0, tiled=True)]
    all_to_all x0 -> x2, waiting for transfers between devices: none -> 48.2 us  [on_device(): lax.all_to_all(jnp.stack([item_half] * lax.axis_size('trow')), 'trow', 0, 0)]
    psum x2, waiting for transfers between devices: 396 us -> 371 us  [on_device(): lax.psum((jnp.dot(users.T, users, precision=lax.Precision.HIGHEST, prefer...]
    all_gather x2, waiting for transfers between devices: 20.3 us -> 0.04 us  [on_device(): user_pool = lax.all_gather(user_half, 'tcol', axis=0, tiled=True)]
    unnamed x14 -> x12, waiting for transfers between devices: 203 us -> 202 us
  transfers between devices with their start and end apart: 14 -> 14, of which waited for: 13 -> 11; matrix products, arithmetic and copies ran while one was open for 15% -> 16% of each run, Pallas kernels for 0% -> 0%
where the time goes in v1:
time: 1000 us; the launch traced here: 992 us
  waiting for transfers between devices  754 us (75%)
  other arithmetic  97.9 us (10%)
  matrix products  56.4 us (6%)
  local copies, waits for them, and re-layouts  40.1 us (4%)
  starting transfers between devices  27.2 us (3%)
  between operations  15.8 us (2%)
    psum x2, waiting for transfers between devices, on_device(): lax.psum((jnp.dot(users.T, users, precision=lax.Precision.HIGHEST, prefer...  371 us
    unnamed x12, waiting for transfers between devices  202 us
    reduce_scatter x2, waiting for transfers between devices, on_device(): lax.psum_scatter(user_pooled, 'tcol', scatter_dimension=0, tiled=True)  112 us
    another operation x12, other arithmetic, precondition(): factor = jnp.linalg.cholesky(gramian)  49.7 us
    all_to_all x2, waiting for transfers between devices, on_device(): lax.all_to_all(jnp.stack([item_half] * lax.axis_size('trow')), 'trow', 0, 0)  48.2 us
    another operation x8, other arithmetic, precondition(): return jax.scipy.linalg.cho_solve((factor, True), gradient.T).T  42.3 us
  transfers between devices with their start and end apart: 14, of which 11 were waited for; matrix products, arithmetic and copies ran while one was open for 16% of the time, Pallas kernels for 0%

profile of v1, /device:TPU:1, one launch (start us, length us, event | category | flops | bytes accessed | tf_op | source)
XLA Modules:
  0.0 991.8 jit_solution(119803367789662200)
XLA Ops:
  7.2 1.8 convert_element_type.69
  9.0 1.4 copy.49
  10.4 7.6 all-to-all-start.2
  19.3 5.0 all-to-all-done.2
  24.3 8.2 all-to-all-start
  33.4 5.7 all-to-all-done
  39.1 1.8 stack.6
  40.9 3.9 all-to-all-start.1
  48.6 21.3 %all-to-all-done.1 = bf16[16,4,128,128]{3,2,1,0:T(8,128)(2,1)S(1)} async-done(((bf16[16,4,128,128]{3,2,1,0:T(8,128)(2,1)}), bf16[16,4,128,128]{3,2,1,0:T(8,128)(2,1)S(1)}, u32[]{:S(2)}, u32[]{:S(2)}) %all-to-all-start.1) | async-done | bytes 2097184 | tf_op jit(solution)/shard_map/all_to_all | solution.py:82
  71.2 2.5 gather_fusion.3
  73.8 3.7 gather_fusion.1
  77.5 4.1 fusion.1
  83.0 2.8 fusion.9
  85.8 4.9 convolution_add_fusion.2
  91.0 2.3 fusion.59
  93.3 2.8 fusion.8
  96.1 4.9 convolution_add_fusion.3
  103.2 1.6 fusion.60
  106.1 97.3 %all-reduce.13.cloned.1.call-done = f32[64,16384]{1,0:T(8,128)} async-done(((f32[64,16384]{1,0:T(8,128)}), f32[64,16384]{1,0:T(8,128)}) %all-reduce.13.cloned.1.call-update) | async-done | bytes 4194320
  205.4 55.9 %reduce-scatter.3.cloned.1.call-done = f32[8,16384]{1,0:T(8,128)} async-done(((f32[64,16384]{1,0:T(8,128)}), f32[8,16384]{1,0:T(8,128)}) %reduce-scatter.3.cloned.1.call-update) | async-done | bytes 524304 | tf_op jit(solution)/shard_map/reduce_scatter | solution.py:92
  261.4 1.9 reshape.384
  264.0 208.9 %all-reduce.19.cloned.1.call-done = (f32[128,128]{0,1:T(8,128)}, f32[128,128]{0,1:T(8,128)}) async-done(((f32[128,128]{0,1:T(8,128)}, f32[128,128]{0,1:T(8,128)}), (f32[128,128]{0,1:T(8,128)}, f32[128,128]{0,1:T(8,128)})) %all-reduce.19.cloned.1.call-update) | async-done | bytes 131088 | tf_op jit(solution)/shard_map/psum | solution.py:61
  475.7 11.7 %cholesky.74 = f32[128,128]{1,0:T(8,128)S(1)} custom-call(f32[128,128]{1,0:T(8,128)S(1)} %get-tuple-element.24), custom_call_target="Cholesky" | custom-call | tf_op jit(solution)/shard_map/jit(cholesky)/cholesky | solution.py:10
  488.8 9.8 custom-call.14
  498.6 10.3 %all-reduce.23.cloned.1.call-done = (f32[128,1024]{0,1:T(8,128)}, f32[128,512]{0,1:T(8,128)}) async-done(((f32[128,1024]{0,1:T(8,128)}, f32[128,512]{0,1:T(8,128)}), (f32[128,1024]{0,1:T(8,128)}, f32[128,512]{0,1:T(8,128)})) %all-reduce.23.cloned.1.call-update) | async-done | bytes 786448 | tf_op jit(solution)/shard_map/psum | solution.py:94
  508.9 1.7 fusion.41
  512.2 11.7 %cholesky.85 = f32[128,128]{1,0:T(8,128)S(1)} custom-call(f32[128,128]{1,0:T(8,128)S(1)} %get-tuple-element.23), custom_call_target="Cholesky" | custom-call | tf_op jit(solution)/shard_map/jit(cholesky)/cholesky | solution.py:10
  525.3 9.9 %custom-call.15 = f32[1,128,128]{1,2,0:T(8,128)S(1)} custom-call(f32[1,128,128]{2,1,0:T(8,128)S(1)} %fusion.25), custom_call_target="InvertDiagBlocksLowerTriangular" | custom-call | tf_op jit(solution)/shard_map/jit(_cho_solve)/triangular_solve | solution.py:11
  536.2 1.8 stack.7
  538.0 6.3 all-to-all-start.3
  546.6 26.9 %all-to-all-done.3 = bf16[16,4,128,128]{3,2,1,0:T(8,128)(2,1)S(1)} async-done(((bf16[16,4,128,128]{3,2,1,0:T(8,128)(2,1)}), bf16[16,4,128,128]{3,2,1,0:T(8,128)(2,1)S(1)}, u32[]{:S(2)}, u32[]{:S(2)}) %all-to-all-start.3) | async-done | bytes 2097184 | tf_op jit(solution)/shard_map/all_to_all | solution.py:82
  574.8 2.5 gather_fusion.5
  577.4 3.7 gather_fusion.4
  581.2 4.1 fusion.3
  586.7 2.8 fusion.11
  589.5 4.9 convolution_add_fusion
  594.4 2.3 fusion.63
  596.7 2.8 fusion.10
  599.5 4.9 convolution_add_fusion.1
  604.6 162.0 %all-reduce.17.cloned.1.call-done = (f32[128,128]{0,1:T(8,128)}, f32[128,128]{0,1:T(8,128)}) async-done(((f32[128,128]{0,1:T(8,128)}, f32[128,128]{0,1:T(8,128)}), (f32[128,128]{0,1:T(8,128)}, f32[128,128]{0,1:T(8,128)})) %all-reduce.17.cloned.1.call-update) | async-done | bytes 131088 | tf_op jit(solution)/shard_map/psum | solution.py:61
  768.5 11.7 %cholesky.96 = f32[128,128]{1,0:T(8,128)S(1)} custom-call(f32[128,128]{1,0:T(8,128)S(1)} %fusion.35), custom_call_target="Cholesky" | custom-call | tf_op jit(solution)/shard_map/jit(cholesky)/cholesky | solution.py:10
  781.0 104.7 %all-reduce.15.cloned.1.call-done = f32[64,16384]{1,0:T(8,128)} async-done(((f32[64,16384]{1,0:T(8,128)}), f32[64,16384]{1,0:T(8,128)}) %all-reduce.15.cloned.1.call-update) | async-done | bytes 4194320
  887.7 56.1 %reduce-scatter.5.cloned.1.call-done = f32[8,16384]{1,0:T(8,128)} async-done(((f32[64,16384]{1,0:T(8,128)}), f32[8,16384]{1,0:T(8,128)}) %reduce-scatter.5.cloned.1.call-update) | async-done | bytes 524304 | tf_op jit(solution)/shard_map/reduce_scatter | solution.py:92
  943.8 1.9 reshape.391
  946.4 9.8 custom-call.16
  956.3 11.7 %cholesky.107 = f32[128,128]{1,0:T(8,128)S(1)} custom-call(f32[128,128]{1,0:T(8,128)S(1)} %fusion.31), custom_call_target="Cholesky" | custom-call | tf_op jit(solution)/shard_map/jit(cholesky)/cholesky | solution.py:10
  969.5 10.0 %custom-call.17 = f32[1,128,128]{1,2,0:T(8,128)S(1)} custom-call(f32[1,128,128]{2,1,0:T(8,128)S(1)} %fusion.27), custom_call_target="InvertDiagBlocksLowerTriangular" | custom-call | tf_op jit(solution)/shard_map/jit(_cho_solve)/triangular_solve | solution.py:11
  979.5 1.7 fusion.33
  (115 shorter events, 37.9 us)
Async XLA Ops:
  7.2 66.6 %all-gather.3.cloned.1.call-start = ((), (), s32[]{:S(2)}) async-start(), calls=%async_computation.6 | async-start | bytes 2359296 | tf_op jit(solution)/shard_map/all_gather | solution.py:80
  10.4 13.9 %all-to-all-start.2 = ((s32[16,1,2]{2,1,0:T(1,128)}), s32[16,1,2]{2,1,0:T(1,128)S(1)}, u32[]{:S(2)}, u32[]{:S(2)}) async-start(s32[16,1,2]{2,1,0:T(1,128)} %copy.49), calls=%async_computation.2 | async-start | bytes 16384 | tf_op jit(solution)/shard_map/all_to_all | solution.py:51
  24.3 14.8 %all-to-all-start = ((s32[8,1,4]{2,1,0:T(1,128)}), s32[8,1,4]{2,1,0:T(1,128)S(1)}, u32[]{:S(2)}, u32[]{:S(2)}) async-start(s32[8,1,4]{2,1,0:T(1,128)} %copy.48), calls=%async_computation | async-start | bytes 8192 | tf_op jit(solution)/shard_map/all_to_all | solution.py:48
  40.9 3.9 copy-start.14
  40.9 4.0 copy-start.13
  40.9 28.9 %all-to-all-start.1 = ((bf16[16,4,128,128]{3,2,1,0:T(8,128)(2,1)}), bf16[16,4,128,128]{3,2,1,0:T(8,128)(2,1)S(1)}, u32[]{:S(2)}, u32[]{:S(2)}) async-start(bf16[16,4,128,128]{3,2,1,0:T(8,128)(2,1)} %stack.6), calls=%async_computation.1 | async-start | bytes 4194304 | tf_op jit(solution)/shard_map/all_to_all | solution.py:82
  44.8 158.7 %all-reduce.13.cloned.1.call-start = ((), (), s32[]{:S(2)}) async-start(), calls=%async_computation.10 | async-start | bytes 8388608
  69.9 1.3 copy-start.4
  73.7 3.8 copy-start.11
  73.7 3.8 copy-start.12
  77.5 4.1 copy-start.1
  81.6 1.4 copy-start.2
  90.7 170.7 %reduce-scatter.3.cloned.1.call-start = ((), (), s32[]{:S(2)}) async-start(), calls=%async_computation.7 | async-start | bytes 4718592 | tf_op jit(solution)/shard_map/reduce_scatter | solution.py:92
  100.9 1.0 copy-start.7
  100.9 2.2 copy-start.6
  100.9 3.9 copy-start.15
  101.0 372.0 %all-reduce.19.cloned.1.call-start = ((), (), s32[]{:S(2)}) async-start(), calls=%async_computation.13 | async-start | bytes 262144 | tf_op jit(solution)/shard_map/psum | solution.py:61
  104.8 404.1 %all-reduce.23.cloned.1.call-start = ((), (), s32[]{:S(2)}) async-start(), calls=%async_computation.15 | async-start | bytes 1572864 | tf_op jit(solution)/shard_map/psum | solution.py:94
  263.3 314.1 %all-gather.5.cloned.1.call-start = ((), (), s32[]{:S(2)}) async-start(), calls=%async_computation.8 | async-start | bytes 2359296 | tf_op jit(solution)/shard_map/all_gather | solution.py:80
  508.9 26.3 %copy-start.9 = (f32[128,512]{0,1:T(8,128)S(1)}, f32[128,512]{0,1:T(8,128)}, u32[]{:S(2)}) copy-start(f32[128,512]{0,1:T(8,128)} %get-tuple-element.18) | copy-start | bytes 786436
  538.0 35.5 %all-to-all-start.3 = ((bf16[16,4,128,128]{3,2,1,0:T(8,128)(2,1)}), bf16[16,4,128,128]{3,2,1,0:T(8,128)(2,1)S(1)}, u32[]{:S(2)}, u32[]{:S(2)}) async-start(bf16[16,4,128,128]{3,2,1,0:T(8,128)(2,1)} %stack.7), calls=%async_computation.4 | async-start | bytes 4194304 | tf_op jit(solution)/shard_map/all_to_all | solution.py:82
  544.3 222.4 %all-reduce.17.cloned.1.call-start = ((), (), s32[]{:S(2)}) async-start(), calls=%async_computation.12 | async-start | bytes 262144 | tf_op jit(solution)/shard_map/psum | solution.py:61
  546.6 339.1 %all-reduce.15.cloned.1.call-start = ((), (), s32[]{:S(2)}) async-start(), calls=%async_computation.11 | async-start | bytes 8388608
  573.5 1.3 copy-start.5
  581.2 4.1 copy-start
  585.3 1.4 copy-start.3
  594.3 349.4 %reduce-scatter.5.cloned.1.call-start = ((), (), s32[]{:S(2)}) async-start(), calls=%async_computation.9 | async-start | bytes 4718592 | tf_op jit(solution)/shard_map/reduce_scatter | solution.py:92
  604.4 375.2 %all-reduce.21.cloned.1.call-start = ((), (), s32[]{:S(2)}) async-start(), calls=%async_computation.14 | async-start | bytes 1572864 | tf_op jit(solution)/shard_map/psum | solution.py:94
  766.7 189.5 %copy-start.8 = (f32[128,128]{0,1:T(8,128)S(1)}, f32[128,128]{0,1:T(8,128)}, u32[]{:S(2)}) copy-start(f32[128,128]{0,1:T(8,128)} %get-tuple-element.12) | copy-start | bytes 196612
  979.5 3.3 copy-start.10
Sparse Core Ops, SparseCore 0:
  10.4 41.2 all-gather.2
  90.8 112.5 all-reduce.12
  206.0 55.3 reduce-scatter.2
  266.8 206.0 all-reduce.18
  476.2 32.6 all-reduce.22
  512.2 38.1 all-gather.4
  556.6 210.0 all-reduce.16
  770.4 115.2 all-reduce.14
  888.4 55.3 reduce-scatter.4
  947.0 29.7 all-reduce.20
